TPU v7x, 32 devices: a whole 2x2x4 slice. The times are simulated.
32 devices in a mesh: blk: 8 (over z, x), grp: 4 (over y, core).
Axes of the slice: x: 2, y: 2, z: 4, core: 2. Of those that a mesh axis runs over, the one named last changes fastest.
Arguments:
- image_student: bfloat16 [8, 4, 256, 768], P('blk', 'grp'), may hold values from -6 to 6
- image_teacher: bfloat16 [8, 4, 256, 1152], P('blk', 'grp'), may hold values from -6 to 6
- text_student: bfloat16 [8, 4, 256, 768], P('blk', 'grp'), may hold values from -6 to 6
- text_teacher: bfloat16 [8, 4, 256, 1152], P('blk', 'grp'), may hold values from -6 to 6
- pair_ids: int32 [8, 4, 256], P('blk', 'grp'), may hold values from 0 to 511
Outputs:
- image_grad: float32 [8, 4, 256, 768], P('blk', 'grp')
- text_grad: float32 [8, 4, 256, 768], P('blk', 'grp')
- bias_grad: float32 [], replicated
All inputs are finite; a program needn't handle non-finite values.
Results may differ from a plain program's by a relative error of at most 0.0021.
Values may be sent and summed in bfloat16 or wider, within the bound.
A program may use at most 64 MiB of HBM per device.

v0:
```python
import math

import jax
import jax.numpy as jnp
from jax import lax
from jax.sharding import PartitionSpec as P

WINDOW = 4


def shifted(array, axis, by):
    count = lax.axis_size(axis)
    return lax.ppermute(array, axis, [(i, (i + by) % count) for i in range(count)])


def text_part(weights, img_stu, scale_s):
    return jnp.einsum("pq,pd->qd", weights, img_stu, preferred_element_type=jnp.float32) * scale_s


def body(image_student, image_teacher, text_student, text_teacher, pair_ids):
    img_stu = image_student[0, 0]
    img_tea = image_teacher[0, 0]
    own_stu = text_student[0, 0]
    own_tea = text_teacher[0, 0]
    own_ids = pair_ids[0, 0]
    scale_s = 2.0 / math.sqrt(img_stu.shape[1])
    scale_t = 2.0 / math.sqrt(img_tea.shape[1])
    arrived = [(own_stu, own_tea, own_ids)]
    current = arrived[0]
    for offset in range(1, WINDOW):
        current = shifted((current[0], current[1], current[2]), "blk", 1)
        arrived.append(current)
    image_grad = jnp.zeros(img_stu.shape, jnp.float32)
    local_total = jnp.float32(0.0)
    weight_list = []
    for offset in range(WINDOW):
        blk_stu, blk_tea, blk_ids = arrived[offset]
        scores = (
            jnp.einsum("pd,qd->pq", img_stu, blk_stu, preferred_element_type=jnp.float32) * scale_s
            - 1.0
        )
        teacher = (
            jnp.einsum("pd,qd->pq", img_tea, blk_tea, preferred_element_type=jnp.float32) * scale_t
            - 1.0
        )
        match = (own_ids[:, None] == blk_ids[None, :]).astype(jnp.float32)
        weights = jax.nn.sigmoid(scores) - 0.5 * jax.nn.sigmoid(teacher) - 0.5 * match
        local_total = local_total + jnp.sum(weights)
        rounded = weights.astype(jnp.bfloat16)
        image_grad = (
            image_grad + jnp.dot(rounded, blk_stu, preferred_element_type=jnp.float32) * scale_s
        )
        weight_list.append(rounded)
    text_grad = text_part(weight_list[0], img_stu, scale_s)
    for offset in range(1, WINDOW):
        recv_weights, recv_images = shifted((weight_list[offset], img_stu), "blk", -offset)
        text_grad = text_grad + text_part(recv_weights, recv_images, scale_s)
    grand_total = lax.psum(local_total, ("blk", "grp"))
    count = float(
        lax.axis_size("blk") * lax.axis_size("grp") * WINDOW * img_stu.shape[0] * img_stu.shape[0]
    )
    return (image_grad[None, None], text_grad[None, None], grand_total / count)


def solution(mesh):
    return jax.shard_map(
        body,
        mesh=mesh,
        in_specs=(
            P("blk", "grp", None, None),
            P("blk", "grp", None, None),
            P("blk", "grp", None, None),
            P("blk", "grp", None, None),
            P("blk", "grp", None),
        ),
        out_specs=(P("blk", "grp", None, None), P("blk", "grp", None, None), P()),
        check_vma=False,
    )
```

profile of v0, /device:TPU:0, one launch (start us, length us, event | category | flops | bytes accessed | tf_op | source)
XLA Modules:
  0.0 155.9 jit_solution(7155952261733519388)
XLA Ops:
  0.6 0.0 copy-start
  0.6 0.0 copy-start.5
  0.7 0.7 copy-done.5
  1.4 3.0 %collective-permute-start.2 = (s32[256]{0:T(256)S(1)}, s32[256]{0:T(256)S(1)}, u32[]{:S(2)}, u32[]{:S(2)}) collective-permute-start(s32[256]{0:T(256)S(1)} %bitcast.68), channel_id=1, source_target_pairs={{0,4},{4,8},{8,12},{12,16},{16,20},{20,24},{24,28},{28,0},{1,5},{5... | collective-permute-start | bytes 3080 | tf_op jit(solution)/shard_map/ppermute | solution.py:13
  4.4 1.5 collective-permute-start
  5.9 1.5 collective-permute-start.1
  7.4 0.0 copy-start.1
  7.4 0.0 copy-start.2
  7.4 3.2 %collective-permute-start.10 = (bf16[256,768]{1,0:T(8,128)(2,1)}, bf16[256,768]{1,0:T(8,128)(2,1)}, u32[]{:S(2)}, u32[]{:S(2)}) collective-permute-start(bf16[256,768]{1,0:T(8,128)(2,1)} %bitcast.64), channel_id=1, source_target_pairs={{0,28},{4,0},{8,4},{12,8},{16,12},{20,16},{24,20},{28,24},{1,29},{... | collective-permute-start | bytes 1179656 | tf_op jit(solution)/shard_map/ppermute | solution.py:13
  10.6 0.0 copy-done
  10.6 1.5 fusion.56
  12.1 0.0 copy-done.1
  12.1 0.0 copy-done.2
  12.1 1.0 fusion.76
  13.1 0.3 fusion.63
  13.4 0.3 fusion.61
  13.7 0.0 collective-permute-done.2
  13.7 0.1 collective-permute-start.5
  13.8 10.4 %collective-permute-done = bf16[256,768]{1,0:T(8,128)(2,1)} collective-permute-done((bf16[256,768]{1,0:T(8,128)(2,1)}, bf16[256,768]{1,0:T(8,128)(2,1)}, u32[]{:S(2)}, u32[]{:S(2)}) %collective-permute-start) | collective-permute-done | bytes 393248 | tf_op jit(solution)/shard_map/ppermute | solution.py:13
  24.1 2.5 %collective-permute-start.3 = (bf16[256,768]{1,0:T(8,128)(2,1)}, bf16[256,768]{1,0:T(8,128)(2,1)S(1)}, u32[]{:S(2)}, u32[]{:S(2)}) collective-permute-start(bf16[256,768]{1,0:T(8,128)(2,1)} %collective-permute-done), channel_id=1, source_target_pairs={{0,4},{4,8},{8,12},{12,16},{16,20},{20,24},{24,28},{28,0},{1,5},{5... | collective-permute-start | bytes 1179656 | tf_op jit(solution)/shard_map/ppermute | solution.py:13
  26.6 10.2 %collective-permute-done.1 = bf16[256,1152]{1,0:T(8,128)(2,1)} collective-permute-done((bf16[256,1152]{1,0:T(8,128)(2,1)}, bf16[256,1152]{1,0:T(8,128)(2,1)}, u32[]{:S(2)}, u32[]{:S(2)}) %collective-permute-start.1) | collective-permute-done | bytes 589856 | tf_op jit(solution)/shard_map/ppermute | solution.py:13
  36.8 1.5 fusion.50
  38.3 2.5 %collective-permute-start.4 = (bf16[256,1152]{1,0:T(8,128)(2,1)}, bf16[256,1152]{1,0:T(8,128)(2,1)}, u32[]{:S(2)}, u32[]{:S(2)}) collective-permute-start(bf16[256,1152]{1,0:T(8,128)(2,1)} %collective-permute-done.1), channel_id=1, source_target_pairs={{0,4},{4,8},{8,12},{12,16},{16,20},{20,24},{24,28},{28,0},{1,5},{5... | collective-permute-start | bytes 1769480 | tf_op jit(solution)/shard_map/ppermute | solution.py:13
  40.8 2.6 %fusion.75 = (f32[]{:T(128)}, bf16[256,256]{1,0:T(8,128)(2,1)}) fusion(s32[256]{0:T(256)S(1)} %collective-permute-done.2, s32[256]{0:T(256)S(1)} %bitcast.70, f32[256,256]{1,0:T(8,128)S(1)} %fusion.50, bf16[256,768]{1,0:T(8,128)(2,1)} %collective-permute-done, bf16[1,1,256,768]{3,2,1,0:T(8,128)(2,1)S(1)} %copy-done.2), kind=kOutput, calls=%fused_computation.88 | convolution fusion | flops 101384192 | bytes 1181700 | tf_op jit(solution)/shard_map/pd,qd->pq/dot_general | solution.py:39
  43.4 2.2 %collective-permute-start.9 = (bf16[256,256]{1,0:T(8,128)(2,1)}, bf16[256,256]{1,0:T(8,128)(2,1)S(1)}, u32[]{:S(2)}, u32[]{:S(2)}) collective-permute-start(bf16[256,256]{1,0:T(8,128)(2,1)} %get-tuple-element.8), channel_id=1, source_target_pairs={{0,28},{4,0},{8,4},{12,8},{16,12},{20,16},{24,20},{28,24},{1,29},{... | collective-permute-start | bytes 393224 | tf_op jit(solution)/shard_map/ppermute | solution.py:13
  45.6 1.3 convolution_add_fusion.4
  48.3 0.0 collective-permute-done.5
  48.3 1.9 %collective-permute-start.14 = (bf16[256,768]{1,0:T(8,128)(2,1)}, bf16[256,768]{1,0:T(8,128)(2,1)}, u32[]{:S(2)}, u32[]{:S(2)}) collective-permute-start(bf16[256,768]{1,0:T(8,128)(2,1)} %bitcast.65), channel_id=1, source_target_pairs={{0,20},{4,24},{8,28},{12,0},{16,4},{20,8},{24,12},{28,16},{1,21},{... | collective-permute-start | bytes 1179656 | tf_op jit(solution)/shard_map/ppermute | solution.py:13
  50.1 18.5 %collective-permute-done.10 = bf16[256,768]{1,0:T(8,128)(2,1)} collective-permute-done((bf16[256,768]{1,0:T(8,128)(2,1)}, bf16[256,768]{1,0:T(8,128)(2,1)}, u32[]{:S(2)}, u32[]{:S(2)}) %collective-permute-start.10) | collective-permute-done | bytes 393248 | tf_op jit(solution)/shard_map/ppermute | solution.py:13
  68.6 1.8 %collective-permute-start.12 = (bf16[256,768]{1,0:T(8,128)(2,1)}, bf16[256,768]{1,0:T(8,128)(2,1)}, u32[]{:S(2)}, u32[]{:S(2)}) collective-permute-start(bf16[256,768]{1,0:T(8,128)(2,1)} %bitcast.66), channel_id=1, source_target_pairs={{0,24},{4,28},{8,0},{12,4},{16,8},{20,12},{24,16},{28,20},{1,25},{... | collective-permute-start | bytes 1179656 | tf_op jit(solution)/shard_map/ppermute | solution.py:13
  70.4 0.6 collective-permute-done.9
  71.0 0.0 collective-permute-start.8
  71.0 1.3 convolution_add_fusion.1
  72.3 0.0 copy-start.3
  72.3 0.0 collective-permute-done.3
  72.3 1.5 collective-permute-start.6
  73.8 0.0 collective-permute-done.4
  73.9 0.1 collective-permute-start.7
  73.9 1.5 fusion.44
  75.4 0.0 copy-done.3
  75.4 1.0 fusion.74
  76.4 0.3 convolution_add_fusion.3
  77.4 0.0 copy-start.4
  77.4 22.8 %collective-permute-done.7 = bf16[256,1152]{1,0:T(8,128)(2,1)} collective-permute-done((bf16[256,1152]{1,0:T(8,128)(2,1)}, bf16[256,1152]{1,0:T(8,128)(2,1)}, u32[]{:S(2)}, u32[]{:S(2)}) %collective-permute-start.7) | collective-permute-done | bytes 589856 | tf_op jit(solution)/shard_map/ppermute | solution.py:13
  100.2 3.4 %collective-permute-start.11 = (bf16[256,256]{1,0:T(8,128)(2,1)S(1)}, bf16[256,256]{1,0:T(8,128)(2,1)S(1)}, u32[]{:S(2)}, u32[]{:S(2)}) collective-permute-start(bf16[256,256]{1,0:T(8,128)(2,1)S(1)} %get-tuple-element.6), channel_id=1, source_target_pairs={{0,24},{4,28},{8,0},{12,4},{16,8},{20,12},{24,16},{28,20},{1,25},{... | collective-permute-start | bytes 393224 | tf_op jit(solution)/shard_map/ppermute | solution.py:13
  103.6 1.5 fusion.38
  105.0 0.0 collective-permute-done.8
  105.0 0.0 collective-permute-done.6
  105.0 0.0 copy-done.4
  105.1 2.0 %fusion.73 = (f32[]{:T(128)}, bf16[256,256]{1,0:T(8,128)(2,1)S(1)}) fusion(s32[256]{0:T(256)S(1)} %collective-permute-done.8, s32[256]{0:T(256)S(1)} %bitcast.72, f32[256,256]{1,0:T(8,128)S(1)} %fusion.38, bf16[256,768]{1,0:T(8,128)(2,1)} %collective-permute-done.6, bf16[1,1,256,768]{3,2,1,0:T(8,128)(2,1)S(1)} %copy-done.4), kind=kOutput, calls=%fused_computation.86 | convolution fusion | flops 101384192 | bytes 1181700 | tf_op jit(solution)/shard_map/pd,qd->pq/dot_general | solution.py:39
  107.7 0.1 collective-permute-start.13
  107.8 40.6 %psum.7 = f32[]{:T(128)} all-reduce(f32[]{:T(128)S(6)} %add.77), channel_id=1, replica_groups=mesh['blk'=8,'grp'=4] {'blk','grp'}, use_global_device_ids=true, to_apply=%region_4.0 | all-reduce | flops 1 | bytes 8 | tf_op jit(solution)/shard_map/psum | solution.py:58
  149.1 2.1 %fusion.4 = f32[1,1,256,768]{3,2,1,0:T(8,128)} fusion(f32[256,768]{1,0:T(8,128)S(1)} %convolution_add_fusion.3, bf16[256,256]{1,0:T(8,128)(2,1)S(1)} %get-tuple-element.4, bf16[256,768]{1,0:T(8,128)(2,1)} %collective-permute-done.6), kind=kOutput, calls=%fused_computation.7 | convolution fusion | flops 101056512 | bytes 2097152 | tf_op jit(solution)/shard_map/dot_general | solution.py:51
  151.2 0.0 collective-permute-done.14
  151.2 0.0 collective-permute-done.13
  151.2 1.3 fusion.77
  152.5 0.0 collective-permute-done.12
  152.5 0.0 collective-permute-done.11
  152.5 2.2 %fusion.2 = f32[1,1,256,768]{3,2,1,0:T(8,128)} fusion(f32[256,768]{1,0:T(8,128)S(1)} %fusion.77, f32[256,768]{1,0:T(8,128)S(1)} %convolution_add_fusion.1, bf16[256,256]{1,0:T(8,128)(2,1)S(1)} %collective-permute-done.11, bf16[256,768]{1,0:T(8,128)(2,1)} %collective-permute-done.12), kind=kOutput, calls=%fused_computation.3 | convolution fusion | flops 101253120 | bytes 2883584 | tf_op jit(solution)/shard_map/pq,pd->qd/dot_general | solution.py:17
Async XLA Ops:
  0.6 10.0 %copy-start = (bf16[1,1,256,1152]{3,2,1,0:T(8,128)(2,1)S(1)}, bf16[1,1,256,1152]{3,2,1,0:T(8,128)(2,1)}, u32[]{:S(2)}) copy-start(bf16[1,1,256,1152]{3,2,1,0:T(8,128)(2,1)} %param.6) | copy-start | bytes 1769476
  0.6 0.7 copy-start.5
  1.4 12.3 %collective-permute-start.2 = (s32[256]{0:T(256)S(1)}, s32[256]{0:T(256)S(1)}, u32[]{:S(2)}, u32[]{:S(2)}) collective-permute-start(s32[256]{0:T(256)S(1)} %bitcast.68), channel_id=1, source_target_pairs={{0,4},{4,8},{8,12},{12,16},{16,20},{20,24},{24,28},{28,0},{1,5},{5... | collective-permute-start | bytes 3080 | tf_op jit(solution)/shard_map/ppermute | solution.py:13
  4.4 19.8 %collective-permute-start = (bf16[256,768]{1,0:T(8,128)(2,1)}, bf16[256,768]{1,0:T(8,128)(2,1)}, u32[]{:S(2)}, u32[]{:S(2)}) collective-permute-start(bf16[256,768]{1,0:T(8,128)(2,1)} %bitcast.63), channel_id=1, source_target_pairs={{0,4},{4,8},{8,12},{12,16},{16,20},{20,24},{24,28},{28,0},{1,5},{5... | collective-permute-start | bytes 1179656 | tf_op jit(solution)/shard_map/ppermute | solution.py:13
  5.9 30.9 %collective-permute-start.1 = (bf16[256,1152]{1,0:T(8,128)(2,1)}, bf16[256,1152]{1,0:T(8,128)(2,1)}, u32[]{:S(2)}, u32[]{:S(2)}) collective-permute-start(bf16[256,1152]{1,0:T(8,128)(2,1)} %bitcast.67), channel_id=1, source_target_pairs={{0,4},{4,8},{8,12},{12,16},{16,20},{20,24},{24,28},{28,0},{1,5},{5... | collective-permute-start | bytes 1769480 | tf_op jit(solution)/shard_map/ppermute | solution.py:13
  7.4 4.7 %copy-start.1 = (bf16[1,1,256,768]{3,2,1,0:T(8,128)(2,1)S(1)}, bf16[1,1,256,768]{3,2,1,0:T(8,128)(2,1)}, u32[]{:S(2)}) copy-start(bf16[1,1,256,768]{3,2,1,0:T(8,128)(2,1)} %param.7) | copy-start | bytes 1179652
  7.4 4.7 %copy-start.2 = (bf16[1,1,256,768]{3,2,1,0:T(8,128)(2,1)S(1)}, bf16[1,1,256,768]{3,2,1,0:T(8,128)(2,1)}, u32[]{:S(2)}) copy-start(bf16[1,1,256,768]{3,2,1,0:T(8,128)(2,1)} %param.5) | copy-start | bytes 1179652
  7.4 61.2 %collective-permute-start.10 = (bf16[256,768]{1,0:T(8,128)(2,1)}, bf16[256,768]{1,0:T(8,128)(2,1)}, u32[]{:S(2)}, u32[]{:S(2)}) collective-permute-start(bf16[256,768]{1,0:T(8,128)(2,1)} %bitcast.64), channel_id=1, source_target_pairs={{0,28},{4,0},{8,4},{12,8},{16,12},{20,16},{24,20},{28,24},{1,29},{... | collective-permute-start | bytes 1179656 | tf_op jit(solution)/shard_map/ppermute | solution.py:13
  13.7 34.6 %collective-permute-start.5 = (s32[256]{0:T(256)S(1)}, s32[256]{0:T(256)S(1)}, u32[]{:S(2)}, u32[]{:S(2)}) collective-permute-start(s32[256]{0:T(256)S(1)} %collective-permute-done.2), channel_id=1, source_target_pairs={{0,4},{4,8},{8,12},{12,16},{16,20},{20,24},{24,28},{28,0},{1,5},{5... | collective-permute-start | bytes 3080 | tf_op jit(solution)/shard_map/ppermute | solution.py:13
  24.1 48.2 %collective-permute-start.3 = (bf16[256,768]{1,0:T(8,128)(2,1)}, bf16[256,768]{1,0:T(8,128)(2,1)S(1)}, u32[]{:S(2)}, u32[]{:S(2)}) collective-permute-start(bf16[256,768]{1,0:T(8,128)(2,1)} %collective-permute-done), channel_id=1, source_target_pairs={{0,4},{4,8},{8,12},{12,16},{16,20},{20,24},{24,28},{28,0},{1,5},{5... | collective-permute-start | bytes 1179656 | tf_op jit(solution)/shard_map/ppermute | solution.py:13
  38.3 35.6 %collective-permute-start.4 = (bf16[256,1152]{1,0:T(8,128)(2,1)}, bf16[256,1152]{1,0:T(8,128)(2,1)}, u32[]{:S(2)}, u32[]{:S(2)}) collective-permute-start(bf16[256,1152]{1,0:T(8,128)(2,1)} %collective-permute-done.1), channel_id=1, source_target_pairs={{0,4},{4,8},{8,12},{12,16},{16,20},{20,24},{24,28},{28,0},{1,5},{5... | collective-permute-start | bytes 1769480 | tf_op jit(solution)/shard_map/ppermute | solution.py:13
  43.4 27.6 %collective-permute-start.9 = (bf16[256,256]{1,0:T(8,128)(2,1)}, bf16[256,256]{1,0:T(8,128)(2,1)S(1)}, u32[]{:S(2)}, u32[]{:S(2)}) collective-permute-start(bf16[256,256]{1,0:T(8,128)(2,1)} %get-tuple-element.8), channel_id=1, source_target_pairs={{0,28},{4,0},{8,4},{12,8},{16,12},{20,16},{24,20},{28,24},{1,29},{... | collective-permute-start | bytes 393224 | tf_op jit(solution)/shard_map/ppermute | solution.py:13
  48.3 102.9 %collective-permute-start.14 = (bf16[256,768]{1,0:T(8,128)(2,1)}, bf16[256,768]{1,0:T(8,128)(2,1)}, u32[]{:S(2)}, u32[]{:S(2)}) collective-permute-start(bf16[256,768]{1,0:T(8,128)(2,1)} %bitcast.65), channel_id=1, source_target_pairs={{0,20},{4,24},{8,28},{12,0},{16,4},{20,8},{24,12},{28,16},{1,21},{... | collective-permute-start | bytes 1179656 | tf_op jit(solution)/shard_map/ppermute | solution.py:13
  68.6 83.9 %collective-permute-start.12 = (bf16[256,768]{1,0:T(8,128)(2,1)}, bf16[256,768]{1,0:T(8,128)(2,1)}, u32[]{:S(2)}, u32[]{:S(2)}) collective-permute-start(bf16[256,768]{1,0:T(8,128)(2,1)} %bitcast.66), channel_id=1, source_target_pairs={{0,24},{4,28},{8,0},{12,4},{16,8},{20,12},{24,16},{28,20},{1,25},{... | collective-permute-start | bytes 1179656 | tf_op jit(solution)/shard_map/ppermute | solution.py:13
  71.0 34.0 %collective-permute-start.8 = (s32[256]{0:T(256)S(1)}, s32[256]{0:T(256)S(1)}, u32[]{:S(2)}, u32[]{:S(2)}) collective-permute-start(s32[256]{0:T(256)S(1)} %collective-permute-done.5), channel_id=1, source_target_pairs={{0,4},{4,8},{8,12},{12,16},{16,20},{20,24},{24,28},{28,0},{1,5},{5... | collective-permute-start | bytes 3080 | tf_op jit(solution)/shard_map/ppermute | solution.py:13
  72.3 3.1 %copy-start.3 = (bf16[1,1,256,768]{3,2,1,0:T(8,128)(2,1)S(1)}, bf16[1,1,256,768]{3,2,1,0:T(8,128)(2,1)}, u32[]{:S(2)}) copy-start(bf16[1,1,256,768]{3,2,1,0:T(8,128)(2,1)} %param.5) | copy-start | bytes 1179652
  72.3 32.7 %collective-permute-start.6 = (bf16[256,768]{1,0:T(8,128)(2,1)S(1)}, bf16[256,768]{1,0:T(8,128)(2,1)}, u32[]{:S(2)}, u32[]{:S(2)}) collective-permute-start(bf16[256,768]{1,0:T(8,128)(2,1)S(1)} %collective-permute-done.3), channel_id=1, source_target_pairs={{0,4},{4,8},{8,12},{12,16},{16,20},{20,24},{24,28},{28,0},{1,5},{5... | collective-permute-start | bytes 1179656 | tf_op jit(solution)/shard_map/ppermute | solution.py:13
  73.9 26.3 %collective-permute-start.7 = (bf16[256,1152]{1,0:T(8,128)(2,1)}, bf16[256,1152]{1,0:T(8,128)(2,1)}, u32[]{:S(2)}, u32[]{:S(2)}) collective-permute-start(bf16[256,1152]{1,0:T(8,128)(2,1)} %collective-permute-done.4), channel_id=1, source_target_pairs={{0,4},{4,8},{8,12},{12,16},{16,20},{20,24},{24,28},{28,0},{1,5},{5... | collective-permute-start | bytes 1769480 | tf_op jit(solution)/shard_map/ppermute | solution.py:13
  77.4 27.7 %copy-start.4 = (bf16[1,1,256,768]{3,2,1,0:T(8,128)(2,1)S(1)}, bf16[1,1,256,768]{3,2,1,0:T(8,128)(2,1)}, u32[]{:S(2)}) copy-start(bf16[1,1,256,768]{3,2,1,0:T(8,128)(2,1)} %param.5) | copy-start | bytes 1179652
  100.2 52.4 %collective-permute-start.11 = (bf16[256,256]{1,0:T(8,128)(2,1)S(1)}, bf16[256,256]{1,0:T(8,128)(2,1)S(1)}, u32[]{:S(2)}, u32[]{:S(2)}) collective-permute-start(bf16[256,256]{1,0:T(8,128)(2,1)S(1)} %get-tuple-element.6), channel_id=1, source_target_pairs={{0,24},{4,28},{8,0},{12,4},{16,8},{20,12},{24,16},{28,20},{1,25},{... | collective-permute-start | bytes 393224 | tf_op jit(solution)/shard_map/ppermute | solution.py:13
  107.7 43.5 %collective-permute-start.13 = (bf16[256,256]{1,0:T(8,128)(2,1)S(1)}, bf16[256,256]{1,0:T(8,128)(2,1)S(1)}, u32[]{:S(2)}, u32[]{:S(2)}) collective-permute-start(bf16[256,256]{1,0:T(8,128)(2,1)S(1)} %get-tuple-element.4), channel_id=1, source_target_pairs={{0,20},{4,24},{8,28},{12,0},{16,4},{20,8},{24,12},{28,16},{1,21},{... | collective-permute-start | bytes 393224 | tf_op jit(solution)/shard_map/ppermute | solution.py:13
where the time goes:
time: 157 us; the launch traced here: 156 us
  waiting for transfers between devices  62.4 us (40%)
  blocking collectives  40.6 us (26%)
  starting transfers between devices  25.2 us (16%)
  matrix products  21.6 us (14%)
  between operations  5.24 us (3%)
    ppermute x15, waiting for transfers between devices, shifted(): lax.ppermute(array, axis, [(i, (i + by) % count) for i in range(count)])  62.4 us
    psum x1, blocking collectives, body(): grand_total = lax.psum(local_total, ('blk', 'grp'))  40.6 us
    ppermute x15, starting transfers between devices, shifted(): lax.ppermute(array, axis, [(i, (i + by) % count) for i in range(count)])  25.2 us
    dot_general x4, matrix products, body(): jnp.einsum('pd,qd->pq', img_stu, blk_stu, preferred_element_type=jnp.floa...  6.62 us
    dot_general x4, matrix products, body(): jnp.einsum('pd,qd->pq', img_tea, blk_tea, preferred_element_type=jnp.floa...  5.85 us
    dot_general x4, matrix products, text_part(): jnp.einsum('pq,pd->qd', weights, img_stu, preferred_element_type=jnp.floa...  5.09 us
    dot_general x4, matrix products, body(): jnp.dot(rounded, blk_stu, preferred_element_type=jnp.float32) * scale_s  4 us
  transfers between devices with their start and end apart: 15, of which 5 were waited for; matrix products, arithmetic and copies ran while one was open for 12% of the time, Pallas kernels for 0%

commit v1 on v0

v1 whole, which is shorter than its diff:
```python
import functools
import math

import jax
import jax.numpy as jnp
from jax import lax
from jax.experimental import pallas as pl
from jax.experimental.pallas import tpu as pltpu
from jax.sharding import PartitionSpec as P

MESH = pl.DeviceIdType.MESH
WINDOW = 4
F_CHUNKS = 4
N_CHUNKS = 4
OUT_CHUNKS = 4


def dot_nt(a, b):
    return lax.dot_general(a, b, (((1,), (1,)), ((), ())), preferred_element_type=jnp.float32)


def dot_tn(a, b):
    return lax.dot_general(a, b, (((0,), (0,)), ((), ())), preferred_element_type=jnp.float32)


def dot_nn(a, b):
    return jnp.dot(a, b, preferred_element_type=jnp.float32)


def fold(w):
    w = jnp.sum(w.reshape(w.shape[0] // 8, 8, w.shape[1]), axis=0)
    out = w[:, 0:128]
    for at in range(128, w.shape[1], 128):
        out = out + w[:, at : at + 128]
    return out


def kernel(
    n_blk,
    n_grp,
    ds,
    inv_count,
    img_stu,
    img_tea,
    txt_stu,
    txt_tea,
    ids,
    out_img,
    out_txt,
    out_bias,
    far,
    near,
    own_ids,
    far_in,
    near_in,
    far_ids_in,
    near_ids_in,
    acc_far,
    acc_near,
    acc_pn,
    pf_out,
    pn_out,
    pf_in,
    pn_in,
    total,
    stage1_own,
    stage1,
    stage2_own,
    stage2,
    local_sem,
    far_send,
    far_recv,
    near_send,
    near_recv,
    ids_send,
    ids_recv,
    pf_send,
    pf_recv,
    pn_send,
    pn_recv,
    s1_send,
    s1_recv,
    s2_send,
    s2_recv,
):
    b = lax.axis_index("blk")
    g = lax.axis_index("grp")
    size = far.shape[0]
    dt = far.shape[1] - ds
    role = lax.rem(g, 2)
    step = 1 - 2 * role
    far_to = lax.rem(b + 2 * step + 2 * n_blk, n_blk)
    far_from = lax.rem(b - 2 * step + 2 * n_blk, n_blk)
    near_to = lax.rem(b - step + n_blk, n_blk)
    near_from = lax.rem(b + step + n_blk, n_blk)

    def at_blk(i):
        return {"blk": i, "grp": g}

    def loads(f_stu, f_tea, n_stu, n_tea):
        return [
            pltpu.make_async_copy(f_stu, far.at[:, pl.ds(0, ds)], local_sem.at[0]),
            pltpu.make_async_copy(f_tea, far.at[:, pl.ds(ds, dt)], local_sem.at[1]),
            pltpu.make_async_copy(n_stu, near.at[:, pl.ds(0, ds)], local_sem.at[2]),
            pltpu.make_async_copy(n_tea, near.at[:, pl.ds(ds, dt)], local_sem.at[3]),
        ]

    @pl.when(role == 0)
    def _():
        for c in loads(txt_stu, txt_tea, img_stu, img_tea):
            c.start()

    @pl.when(role == 1)
    def _():
        for c in loads(img_stu, img_tea, txt_stu, txt_tea):
            c.start()

    ids_load = pltpu.make_async_copy(ids, own_ids, local_sem.at[4])
    ids_load.start()

    barrier = pltpu.get_barrier_semaphore()
    for k in range(1, n_blk):
        pl.semaphore_signal(
            barrier, inc=1, device_id=at_blk(lax.rem(b + k, n_blk)), device_id_type=MESH
        )
    for k in range(1, n_grp):
        pl.semaphore_signal(
            barrier,
            inc=1,
            device_id={"blk": b, "grp": lax.rem(g + k, n_grp)},
            device_id_type=MESH,
        )
    for c in loads(txt_stu, txt_tea, img_stu, img_tea):
        c.wait()
    ids_load.wait()
    pl.semaphore_wait(barrier, n_blk - 1 + n_grp - 1)

    def remote(src, dst, send, recv, to):
        return pltpu.make_async_remote_copy(
            src_ref=src, dst_ref=dst, send_sem=send, recv_sem=recv,
            device_id=to, device_id_type=MESH,
        )

    fr = size // F_CHUNKS
    nr = size // N_CHUNKS
    ids_f = remote(own_ids, far_ids_in, ids_send.at[0], ids_recv.at[0], at_blk(far_to))
    ids_n = remote(own_ids, near_ids_in, ids_send.at[1], ids_recv.at[1], at_blk(near_to))
    ids_n.start()
    ids_f.start()
    near_copies = [
        remote(
            near.at[pl.ds(j * nr, nr)], near_in.at[pl.ds(j * nr, nr)],
            near_send.at[j], near_recv.at[j], at_blk(near_to),
        )
        for j in range(N_CHUNKS)
    ]
    far_copies = [
        remote(
            far.at[pl.ds(i * fr, fr)], far_in.at[pl.ds(i * fr, fr)],
            far_send.at[i], far_recv.at[i], at_blk(far_to),
        )
        for i in range(F_CHUNKS)
    ]
    for c in near_copies:
        c.start()
    for c in far_copies:
        c.start()

    scale_s = 2.0 / math.sqrt(ds)
    scale_t = 2.0 / math.sqrt(dt)

    def as_column(row):
        return jnp.transpose(jnp.broadcast_to(row, (128, row.shape[1])))[:, 0:1]

    def weigh(f, n, f_id, n_id):
        s = dot_nt(f[:, :ds], n[:, :ds]) * (0.5 * scale_s) - 0.5
        q = dot_nt(f[:, ds:], n[:, ds:]) * (0.5 * scale_t) - 0.5
        shift = jnp.where(f_id == n_id, -0.25, 0.25)
        return 0.5 * jnp.tanh(s) - 0.25 * jnp.tanh(q) + shift

    own_row = own_ids[...]
    own_col = as_column(own_row)

    w = weigh(far[...], near[...], own_col, own_row)
    total[...] = fold(w)
    wb = w.astype(jnp.bfloat16)
    acc_far[...] = dot_nn(wb, near[:, :ds])
    acc_near[...] = dot_tn(wb, far[:, :ds])

    ids_n.wait_recv()
    near_row = near_ids_in[...]
    for j in range(N_CHUNKS):
        near_copies[j].wait_recv()
        rows = pl.ds(j * nr, nr)
        w = weigh(near_in[rows, :], far[...], as_column(near_row)[j * nr : (j + 1) * nr], own_row)
        total[...] += fold(w)
        wb = w.astype(jnp.bfloat16)
        acc_far[...] += dot_tn(wb, near_in[rows, pl.ds(0, ds)])
        acc_pn[rows, :] = dot_nn(wb, far[:, :ds])

    ids_f.wait_recv()
    far_col = as_column(far_ids_in[...])
    pf_copies = []
    for i in range(F_CHUNKS):
        far_copies[i].wait_recv()
        rows = pl.ds(i * fr, fr)
        f = far_in[rows, :]
        f_id = far_col[i * fr : (i + 1) * fr]
        w1 = weigh(f, near[...], f_id, own_row)
        w2 = weigh(f, near_in[...], f_id, near_row)
        total[...] += fold(w1) + fold(w2)
        w1 = w1.astype(jnp.bfloat16)
        w2 = w2.astype(jnp.bfloat16)
        back = dot_nn(w1, near[:, :ds]) + dot_nn(w2, near_in[:, :ds])
        pf_out[rows, :] = (back * scale_s).astype(jnp.bfloat16)
        c = remote(
            pf_out.at[rows], pf_in.at[rows], pf_send.at[i], pf_recv.at[i], at_blk(far_from)
        )
        c.start()
        pf_copies.append(c)
        acc_near[...] += dot_tn(w1, f[:, :ds])
        acc_pn[...] += dot_tn(w2, f[:, :ds])

    stage1_own[...] = total[...]
    stage1[pl.ds(b, 1)] = total[...][None]
    s1 = []
    for k in range(1, n_blk):
        c = remote(
            stage1_own, stage1.at[b], s1_send.at[k - 1], s1_recv.at[k - 1],
            at_blk(lax.rem(b + k, n_blk)),
        )
        c.start()
        s1.append(c)

    pr = size // OUT_CHUNKS
    pn_copies = []
    for j in range(OUT_CHUNKS):
        rows = pl.ds(j * pr, pr)
        pn_out[rows, :] = (acc_pn[rows, :] * scale_s).astype(jnp.bfloat16)
        c = remote(
            pn_out.at[rows], pn_in.at[rows], pn_send.at[j], pn_recv.at[j], at_blk(near_from)
        )
        c.start()
        pn_copies.append(c)

    for c in s1:
        c.wait_recv()
    part = stage1[0]
    for k in range(1, n_blk):
        part = part + stage1[k]
    stage2_own[...] = part
    stage2[pl.ds(g, 1)] = part[None]
    s2 = []
    for k in range(1, n_grp):
        c = remote(
            stage2_own, stage2.at[g], s2_send.at[k - 1], s2_recv.at[k - 1],
            {"blk": b, "grp": lax.rem(g + k, n_grp)},
        )
        c.start()
        s2.append(c)

    def finish(copies, acc, arrived, rows_each, out_a, out_b):
        for i, c in enumerate(copies):
            c.wait_recv()
            rows = pl.ds(i * rows_each, rows_each)
            value = acc[rows, :] * scale_s + arrived[rows, :].astype(jnp.float32)

            @pl.when(role == 0)
            def _():
                out_a[rows, :] = value

            @pl.when(role == 1)
            def _():
                out_b[rows, :] = value

    finish(pf_copies, acc_far, pf_in, fr, out_txt, out_img)
    finish(pn_copies, acc_near, pn_in, pr, out_img, out_txt)

    for c in s2:
        c.wait_recv()
    whole = stage2[0]
    for k in range(1, n_grp):
        whole = whole + stage2[k]
    out_bias[0, 0] = jnp.sum(whole) * inv_count

    for c in [ids_f, ids_n] + near_copies + far_copies + pf_copies + pn_copies + s1 + s2:
        c.wait_send()


def solution(mesh):
    n_blk, n_grp = mesh.shape["blk"], mesh.shape["grp"]

    def body(image_student, image_teacher, text_student, text_teacher, pair_ids):
        size, ds = image_student.shape[2:]
        dt = image_teacher.shape[3]
        bf, f32 = jnp.bfloat16, jnp.float32
        dma = lambda k: pltpu.SemaphoreType.DMA((max(k, 1),))
        count = float(n_blk * n_grp * WINDOW * size * size)
        img, txt, bias = pl.pallas_call(
            functools.partial(kernel, n_blk, n_grp, ds, 1.0 / count),
            out_shape=(
                jax.ShapeDtypeStruct((size, ds), f32),
                jax.ShapeDtypeStruct((size, ds), f32),
                jax.ShapeDtypeStruct((1, 1), f32),
            ),
            in_specs=[pl.BlockSpec(memory_space=pl.ANY)] * 5,
            out_specs=(
                pl.BlockSpec(memory_space=pltpu.VMEM),
                pl.BlockSpec(memory_space=pltpu.VMEM),
                pl.BlockSpec(memory_space=pltpu.SMEM),
            ),
            scratch_shapes=[
                pltpu.VMEM((size, ds + dt), bf),
                pltpu.VMEM((size, ds + dt), bf),
                pltpu.VMEM((1, size), jnp.int32),
                pltpu.VMEM((size, ds + dt), bf),
                pltpu.VMEM((size, ds + dt), bf),
                pltpu.VMEM((1, size), jnp.int32),
                pltpu.VMEM((1, size), jnp.int32),
                pltpu.VMEM((size, ds), f32),
                pltpu.VMEM((size, ds), f32),
                pltpu.VMEM((size, ds), f32),
                pltpu.VMEM((size, ds), bf),
                pltpu.VMEM((size, ds), bf),
                pltpu.VMEM((size, ds), bf),
                pltpu.VMEM((size, ds), bf),
                pltpu.VMEM((8, 128), f32),
                pltpu.VMEM((8, 128), f32),
                pltpu.VMEM((n_blk, 8, 128), f32),
                pltpu.VMEM((8, 128), f32),
                pltpu.VMEM((n_grp, 8, 128), f32),
                dma(5),
                dma(F_CHUNKS),
                dma(F_CHUNKS),
                dma(N_CHUNKS),
                dma(N_CHUNKS),
                dma(2),
                dma(2),
                dma(F_CHUNKS),
                dma(F_CHUNKS),
                dma(OUT_CHUNKS),
                dma(OUT_CHUNKS),
                dma(n_blk - 1),
                dma(n_blk - 1),
                dma(n_grp - 1),
                dma(n_grp - 1),
            ],
            compiler_params=pltpu.CompilerParams(
                collective_id=0, has_side_effects=True, vmem_limit_bytes=40 * 1024 * 1024
            ),
        )(
            image_student[0, 0],
            image_teacher[0, 0],
            text_student[0, 0],
            text_teacher[0, 0],
            pair_ids[0],
        )
        return img[None, None], txt[None, None], bias[0, 0]

    return jax.shard_map(
        body,
        mesh=mesh,
        in_specs=(
            P("blk", "grp", None, None),
            P("blk", "grp", None, None),
            P("blk", "grp", None, None),
            P("blk", "grp", None, None),
            P("blk", "grp", None),
        ),
        out_specs=(P("blk", "grp", None, None), P("blk", "grp", None, None), P()),
        check_vma=False,
    )
```

time: 157 us -> 65.8 us (0.42)
  waiting for transfers between devices: 62.4 us -> 0 us
  Pallas kernels: 0 us -> 56.6 us
  blocking collectives: 40.6 us -> 0 us
  starting transfers between devices: 25.2 us -> 0 us
  matrix products: 21.6 us -> 0 us
  local copies, waits for them, and re-layouts: 0.76 us -> 6.55 us
  between operations: 5.24 us -> 2.34 us
    ppermute x15 -> x0, waiting for transfers between devices: 62.4 us -> none  [shifted(): lax.ppermute(array, axis, [(i, (i + by) % count) for i in range(count)])]
    pallas_call x0 -> x1, Pallas kernels: none -> 56.6 us  [body(): pl.pallas_call(functools.partial(kernel, n_blk, n_grp, ds, 1.0 / count),...]
    psum x1 -> x0, blocking collectives: 40.6 us -> none  [body(): grand_total = lax.psum(local_total, ('blk', 'grp'))]
    ppermute x15 -> x0, starting transfers between devices: 25.2 us -> none  [shifted(): lax.ppermute(array, axis, [(i, (i + by) % count) for i in range(count)])]
    dot_general x16 -> x0, matrix products: 21.6 us -> none  [the longest x4 6.62 us: body(): jnp.einsum('pd,qd->pq', img_stu, blk_stu, preferred_element_type=jnp.floa...]
    unnamed x12, local copies, waits for them, and re-layouts: 0.76 us -> 6.55 us
  transfers between devices with their start and end apart: 15 -> 0, of which waited for: 5 -> 0; matrix products, arithmetic and copies ran while one was open for 12% -> 0% of each run, Pallas kernels for 0% -> 0%
where the time goes in v1:
time: 65.8 us; the launch traced here: 65.5 us
  Pallas kernels  56.6 us (86%)
  local copies, waits for them, and re-layouts  6.55 us (10%)
  between operations  2.34 us (4%)
    pallas_call x1, Pallas kernels, body(): pl.pallas_call(functools.partial(kernel, n_blk, n_grp, ds, 1.0 / count),...  56.6 us
    unnamed x12, local copies, waits for them, and re-layouts  6.55 us

profile of v1, /device:TPU:0, one launch (start us, length us, event | category | flops | bytes accessed | tf_op | source)
XLA Modules:
  0.0 65.5 jit_solution(14861380477692307703)
XLA Ops:
  0.6 0.0 copy-start.4
  0.6 0.7 %copy-done.4 = s32[1,1,256]{2,1,0:T(1,128)S(1)} copy-done((s32[1,1,256]{2,1,0:T(1,128)S(1)}, s32[1,1,256]{2,1,0:T(1,128)}, u32[]{:S(2)}) %copy-start.4) | copy-done | bytes 1048
  1.3 0.0 copy-start
  1.3 1.1 %copy-done = bf16[1,1,256,1152]{3,2,1,0:T(8,128)(2,1)S(1)} copy-done((bf16[1,1,256,1152]{3,2,1,0:T(8,128)(2,1)S(1)}, bf16[1,1,256,1152]{3,2,1,0:T(8,128)(2,1)}, u32[]{:S(2)}) %copy-start) | copy-done | bytes 589848
  2.4 0.0 copy-start.1
  2.4 1.1 %copy-done.1 = bf16[1,1,256,1152]{3,2,1,0:T(8,128)(2,1)S(1)} copy-done((bf16[1,1,256,1152]{3,2,1,0:T(8,128)(2,1)S(1)}, bf16[1,1,256,1152]{3,2,1,0:T(8,128)(2,1)}, u32[]{:S(2)}) %copy-start.1) | copy-done | bytes 589848
  3.4 0.0 copy-start.2
  3.4 1.0 %copy-done.2 = bf16[1,1,256,768]{3,2,1,0:T(8,128)(2,1)S(1)} copy-done((bf16[1,1,256,768]{3,2,1,0:T(8,128)(2,1)S(1)}, bf16[1,1,256,768]{3,2,1,0:T(8,128)(2,1)}, u32[]{:S(2)}) %copy-start.2) | copy-done | bytes 393240
  4.4 0.0 copy-start.3
  4.4 1.0 %copy-done.3 = bf16[1,1,256,768]{3,2,1,0:T(8,128)(2,1)S(1)} copy-done((bf16[1,1,256,768]{3,2,1,0:T(8,128)(2,1)S(1)}, bf16[1,1,256,768]{3,2,1,0:T(8,128)(2,1)}, u32[]{:S(2)}) %copy-start.3) | copy-done | bytes 393240
  5.4 56.6 %shard_map.76 = (f32[256,768]{1,0:T(8,128)S(1)}, f32[256,768]{1,0:T(8,128)S(1)}, f32[1,1]{1,0:T(1,128)}) custom-call(bf16[256,768]{1,0:T(8,128)(2,1)S(1)} %bitcast.12, bf16[256,1152]{1,0:T(8,128)(2,1)S(1)} %bitcast.10, bf16[256,768]{1,0:T(8,128)(2,1)S(1)} %bitcast.13, bf16[256,1152]{1,0:T(8,128)(2,1)S(1)} %bitcast.11, s32[1,256]{1,0:T(1,128)S(1)} %bitcast.14), custom_call_target="tpu_custom_call" | custom-call | tf_op jit(solution)/shard_map/pallas_call | solution.py:299
  62.0 0.9 %copy.11 = f32[1,1,256,768]{3,2,1,0:T(8,128)} copy(f32[1,1,256,768]{3,2,1,0:T(8,128)S(1)} %bitcast.9) | data formatting | bytes 1572864
  62.9 0.9 %copy.12 = f32[1,1,256,768]{3,2,1,0:T(8,128)} copy(f32[1,1,256,768]{3,2,1,0:T(8,128)S(1)} %bitcast.8) | data formatting | bytes 1572864
Async XLA Ops:
  0.6 0.7 %copy-start.4 = (s32[1,1,256]{2,1,0:T(1,128)S(1)}, s32[1,1,256]{2,1,0:T(1,128)}, u32[]{:S(2)}) copy-start(s32[1,1,256]{2,1,0:T(1,128)} %param.9) | copy-start | bytes 3076
  1.3 1.1 %copy-start = (bf16[1,1,256,1152]{3,2,1,0:T(8,128)(2,1)S(1)}, bf16[1,1,256,1152]{3,2,1,0:T(8,128)(2,1)}, u32[]{:S(2)}) copy-start(bf16[1,1,256,1152]{3,2,1,0:T(8,128)(2,1)} %param.6) | copy-start | bytes 1769476
  2.4 1.1 %copy-start.1 = (bf16[1,1,256,1152]{3,2,1,0:T(8,128)(2,1)S(1)}, bf16[1,1,256,1152]{3,2,1,0:T(8,128)(2,1)}, u32[]{:S(2)}) copy-start(bf16[1,1,256,1152]{3,2,1,0:T(8,128)(2,1)} %param.8) | copy-start | bytes 1769476
  3.4 1.0 %copy-start.2 = (bf16[1,1,256,768]{3,2,1,0:T(8,128)(2,1)S(1)}, bf16[1,1,256,768]{3,2,1,0:T(8,128)(2,1)}, u32[]{:S(2)}) copy-start(bf16[1,1,256,768]{3,2,1,0:T(8,128)(2,1)} %param.5) | copy-start | bytes 1179652
  4.4 1.0 %copy-start.3 = (bf16[1,1,256,768]{3,2,1,0:T(8,128)(2,1)S(1)}, bf16[1,1,256,768]{3,2,1,0:T(8,128)(2,1)}, u32[]{:S(2)}) copy-start(bf16[1,1,256,768]{3,2,1,0:T(8,128)(2,1)} %param.7) | copy-start | bytes 1179652

commit v2 on v1

--- a/solution.py
+++ b/solution.py
@@ -346,7 +346,7 @@
                 dma(n_grp - 1),
             ],
             compiler_params=pltpu.CompilerParams(
-                collective_id=0, has_side_effects=True, vmem_limit_bytes=40 * 1024 * 1024
+                collective_id=0, has_side_effects=True, vmem_limit_bytes=62 * 1024 * 1024
             ),
         )(
             image_student[0, 0],

time: 65.8 us -> 62.7 us (0.953)
  local copies, waits for them, and re-layouts: 6.55 us -> 3.02 us
    unnamed x12 -> x4, local copies, waits for them, and re-layouts: 6.55 us -> 3.02 us
where the time goes in v2:
time: 62.7 us; the launch traced here: 62.5 us
  Pallas kernels  57 us (91%)
  local copies, waits for them, and re-layouts  3.02 us (5%)
  between operations  2.41 us (4%)
    pallas_call x1, Pallas kernels, body(): pl.pallas_call(functools.partial(kernel, n_blk, n_grp, ds, 1.0 / count),...  57 us
    unnamed x4, local copies, waits for them, and re-layouts  3.02 us

profile of v2, /device:TPU:0, one launch (start us, length us, event | category | flops | bytes accessed | tf_op | source)
XLA Modules:
  0.0 62.5 jit_solution(17568228614895481168)
XLA Ops:
  0.6 57.0 %shard_map.76 = (f32[256,768]{1,0:T(8,128)}, f32[256,768]{1,0:T(8,128)}, f32[1,1]{1,0:T(1,128)}) custom-call(bf16[256,768]{1,0:T(8,128)(2,1)} %bitcast.12, bf16[256,1152]{1,0:T(8,128)(2,1)} %bitcast.10, bf16[256,768]{1,0:T(8,128)(2,1)} %bitcast.13, bf16[256,1152]{1,0:T(8,128)(2,1)} %bitcast.11, s32[1,256]{1,0:T(1,128)} %bitcast.14), custom_call_target="tpu_custom_call" | custom-call | tf_op jit(solution)/shard_map/pallas_call | solution.py:299
  57.7 0.0 copy-start
  57.7 2.1 %copy.11 = f32[1,1,256,768]{3,2,1,0:T(8,128)} copy(f32[1,1,256,768]{3,2,1,0:T(8,128)} %bitcast.9) | data formatting | bytes 1572864
  59.8 0.0 copy-done
  59.8 0.9 %copy.12 = f32[1,1,256,768]{3,2,1,0:T(8,128)} copy(f32[1,1,256,768]{3,2,1,0:T(8,128)S(1)} %bitcast.8) | data formatting | bytes 1572864
Async XLA Ops:
  57.7 2.1 %copy-start = (f32[256,768]{1,0:T(8,128)S(1)}, f32[256,768]{1,0:T(8,128)}, u32[]{:S(2)}) copy-start(f32[256,768]{1,0:T(8,128)} %get-tuple-element.7) | copy-start | bytes 2359300

commit v3 on v2

--- a/solution.py
+++ b/solution.py
@@ -82,6 +82,7 @@
     s1_recv,
     s2_send,
     s2_recv,
+    out_sem,
 ):
     b = lax.axis_index("blk")
     g = lax.axis_index("grp")
@@ -198,6 +199,19 @@
         acc_far[...] += dot_tn(wb, near_in[rows, pl.ds(0, ds)])
         acc_pn[rows, :] = dot_nn(wb, far[:, :ds])
 
+    def share_total():
+        stage1_own[...] = total[...]
+        stage1[pl.ds(b, 1)] = total[...][None]
+        s1 = []
+        for k in range(1, n_blk):
+            c = remote(
+                stage1_own, stage1.at[b], s1_send.at[k - 1], s1_recv.at[k - 1],
+                at_blk(lax.rem(b + k, n_blk)),
+            )
+            c.start()
+            s1.append(c)
+        return s1
+
     ids_f.wait_recv()
     far_col = as_column(far_ids_in[...])
     pf_copies = []
@@ -209,6 +223,8 @@
         w1 = weigh(f, near[...], f_id, own_row)
         w2 = weigh(f, near_in[...], f_id, near_row)
         total[...] += fold(w1) + fold(w2)
+        if i == F_CHUNKS - 1:
+            s1 = share_total()
         w1 = w1.astype(jnp.bfloat16)
         w2 = w2.astype(jnp.bfloat16)
         back = dot_nn(w1, near[:, :ds]) + dot_nn(w2, near_in[:, :ds])
@@ -220,17 +236,6 @@
         pf_copies.append(c)
         acc_near[...] += dot_tn(w1, f[:, :ds])
         acc_pn[...] += dot_tn(w2, f[:, :ds])
-
-    stage1_own[...] = total[...]
-    stage1[pl.ds(b, 1)] = total[...][None]
-    s1 = []
-    for k in range(1, n_blk):
-        c = remote(
-            stage1_own, stage1.at[b], s1_send.at[k - 1], s1_recv.at[k - 1],
-            at_blk(lax.rem(b + k, n_blk)),
-        )
-        c.start()
-        s1.append(c)
 
     pr = size // OUT_CHUNKS
     pn_copies = []
@@ -259,22 +264,27 @@
         c.start()
         s2.append(c)
 
-    def finish(copies, acc, arrived, rows_each, out_a, out_b):
+    written = []
+
+    def finish(copies, acc, arrived, rows_each, out_a, out_b, first):
         for i, c in enumerate(copies):
             c.wait_recv()
             rows = pl.ds(i * rows_each, rows_each)
-            value = acc[rows, :] * scale_s + arrived[rows, :].astype(jnp.float32)
+            acc[rows, :] = acc[rows, :] * scale_s + arrived[rows, :].astype(jnp.float32)
+            put_a = pltpu.make_async_copy(acc.at[rows], out_a.at[rows], out_sem.at[first + i])
+            put_b = pltpu.make_async_copy(acc.at[rows], out_b.at[rows], out_sem.at[first + i])
+            written.append(put_a)
 
             @pl.when(role == 0)
             def _():
-                out_a[rows, :] = value
+                put_a.start()
 
             @pl.when(role == 1)
             def _():
-                out_b[rows, :] = value
-
-    finish(pf_copies, acc_far, pf_in, fr, out_txt, out_img)
-    finish(pn_copies, acc_near, pn_in, pr, out_img, out_txt)
+                put_b.start()
+
+    finish(pf_copies, acc_far, pf_in, fr, out_txt, out_img, 0)
+    finish(pn_copies, acc_near, pn_in, pr, out_img, out_txt, F_CHUNKS)
 
     for c in s2:
         c.wait_recv()
@@ -283,8 +293,29 @@
         whole = whole + stage2[k]
     out_bias[0, 0] = jnp.sum(whole) * inv_count
 
+    for c in written:
+        c.wait()
     for c in [ids_f, ids_n] + near_copies + far_copies + pf_copies + pn_copies + s1 + s2:
         c.wait_send()
+
+
+def land(a, b, out_a, out_b, held, came, went):
+    each = a.shape[0] // OUT_CHUNKS
+    pieces = [(at, i) for i in range(OUT_CHUNKS) for at in range(2)]
+    arrays = ((a, out_a), (b, out_b))
+    ins, outs = [], []
+    for at, i in pieces:
+        rows = pl.ds(i * each, each)
+        src, dst = arrays[at]
+        ins.append(pltpu.make_async_copy(src.at[rows], held.at[at, rows], came.at[at, i]))
+        outs.append(pltpu.make_async_copy(held.at[at, rows], dst.at[rows], went.at[at, i]))
+    for c in ins:
+        c.start()
+    for c, d in zip(ins, outs):
+        c.wait()
+        d.start()
+    for d in outs:
+        d.wait()
 
 
 def solution(mesh):
@@ -305,8 +336,8 @@
             ),
             in_specs=[pl.BlockSpec(memory_space=pl.ANY)] * 5,
             out_specs=(
-                pl.BlockSpec(memory_space=pltpu.VMEM),
-                pl.BlockSpec(memory_space=pltpu.VMEM),
+                pl.BlockSpec(memory_space=pl.ANY),
+                pl.BlockSpec(memory_space=pl.ANY),
                 pl.BlockSpec(memory_space=pltpu.SMEM),
             ),
             scratch_shapes=[
@@ -344,6 +375,7 @@
                 dma(n_blk - 1),
                 dma(n_grp - 1),
                 dma(n_grp - 1),
+                dma(F_CHUNKS + OUT_CHUNKS),
             ],
             compiler_params=pltpu.CompilerParams(
                 collective_id=0, has_side_effects=True, vmem_limit_bytes=62 * 1024 * 1024
@@ -355,6 +387,21 @@
             text_teacher[0, 0],
             pair_ids[0],
         )
+        img, txt = pl.pallas_call(
+            land,
+            out_shape=(
+                jax.ShapeDtypeStruct((size, ds), f32),
+                jax.ShapeDtypeStruct((size, ds), f32),
+            ),
+            in_specs=[pl.BlockSpec(memory_space=pl.ANY)] * 2,
+            out_specs=[pl.BlockSpec(memory_space=pl.ANY)] * 2,
+            scratch_shapes=[
+                pltpu.VMEM((2, size, ds), f32),
+                pltpu.SemaphoreType.DMA((2, OUT_CHUNKS)),
+                pltpu.SemaphoreType.DMA((2, OUT_CHUNKS)),
+            ],
+            compiler_params=pltpu.CompilerParams(vmem_limit_bytes=62 * 1024 * 1024),
+        )(img, txt)
         return img[None, None], txt[None, None], bias[0, 0]
 
     return jax.shard_map(

time: 62.7 us -> 60.6 us (0.967)
  local copies, waits for them, and re-layouts: 3.02 us -> 0 us
  Pallas kernels: 57 us -> 57.8 us
    unnamed x4 -> x0, local copies, waits for them, and re-layouts: 3.02 us -> none
    pallas_call x0 -> x1, Pallas kernels: none -> 2.29 us  [body(): pl.pallas_call(land, out_shape=(jax.ShapeDtypeStruct((size, ds), f32), ja...]
    pallas_call x1, Pallas kernels: 57 us -> 55.5 us  [body(): pl.pallas_call(functools.partial(kernel, n_blk, n_grp, ds, 1.0 / count),...]
where the time goes in v3:
time: 60.6 us; the launch traced here: 60.2 us
  Pallas kernels  57.8 us (95%)
  between operations  2.41 us (4%)
    pallas_call x1, Pallas kernels, body(): pl.pallas_call(functools.partial(kernel, n_blk, n_grp, ds, 1.0 / count),...  55.5 us
    pallas_call x1, Pallas kernels, body(): pl.pallas_call(land, out_shape=(jax.ShapeDtypeStruct((size, ds), f32), ja...  2.29 us

profile of v3, /device:TPU:0, one launch (start us, length us, event | category | flops | bytes accessed | tf_op | source)
XLA Modules:
  0.0 60.2 jit_solution(15344508574759662210)
XLA Ops:
  0.6 55.5 %shard_map.76 = (f32[256,768]{1,0:T(8,128)}, f32[256,768]{1,0:T(8,128)}, f32[1,1]{1,0:T(1,128)}) custom-call(bf16[256,768]{1,0:T(8,128)(2,1)} %bitcast.10, bf16[256,1152]{1,0:T(8,128)(2,1)} %bitcast.8, bf16[256,768]{1,0:T(8,128)(2,1)} %bitcast.11, bf16[256,1152]{1,0:T(8,128)(2,1)} %bitcast.9, s32[1,256]{1,0:T(1,128)} %bitcast.12), custom_call_target="tpu_custom_call" | custom-call | tf_op jit(solution)/shard_map/pallas_call | solution.py:330
  56.2 2.3 %shard_map.77 = (f32[256,768]{1,0:T(8,128)}, f32[256,768]{1,0:T(8,128)}) custom-call(f32[256,768]{1,0:T(8,128)} %get-tuple-element.8.a, f32[256,768]{1,0:T(8,128)} %get-tuple-element.9.b), custom_call_target="tpu_custom_call" | custom-call | tf_op jit(solution)/shard_map/pallas_call | solution.py:390
